TPU v7x, 32 devices: a whole 2x2x4 slice. The times are simulated.
32 devices in a mesh: groups: 2 (over y), space: 16 (over z, x, core).
Axes of the slice: x: 2, y: 2, z: 4, core: 2. Of those that a mesh axis runs over, the one named last changes fastest.
Arguments:
- wavefield: bfloat16 [8192, 1024], P(('groups', 'space')), parts along dimension 0, may hold values from -6 to 6
- redatum_taps: float32 [512, 65], P('groups'), parts along dimension 0, may hold values from -0.75 to 0.75
- cell_x: int32 [5, 16384], replicated, may hold values from 0 to 4095
- cell_depth: int32 [16384], replicated, may hold values from 1 to 511
- slowness: float32 [4], replicated, may hold values from 0.02 to 0.2
- illumination: float32 [32768], P('groups'), parts along dimension 0, may hold values from 0.3 to 3
- aperture: int32 [8192, 1024], P(('groups', 'space')), parts along dimension 0, may hold values 0 or 1
Outputs:
- image: float32 [32, 1024], P(('groups', 'space')), parts along dimension 0
There are 2 independent parts, one for each index of `groups`. A program takes and returns all parts, laid end to end along the dimension named above; an argument that names none is the same for every part. Nothing has to cross between parts.
All inputs are finite; a program needn't handle non-finite values. No bound on the sum of `aperture` on one device may be relied on, other than what follows from the above.
Results may differ from a plain program's by a relative error of at most 0.0075.
Values may be sent and summed in bfloat16 or wider, within the bound.
A program may use at most 64 MiB of HBM per device.

v0:
```python
import functools
import math

import jax
import jax.numpy as jnp
from jax import lax
from jax.experimental import pallas as pl
from jax.experimental.pallas import tpu as pltpu
from jax.sharding import PartitionSpec as P

LEVELS = 4
BOXES = 16
LANES = 128
COLUMNS = 256
TILE = 64
SINE = (3.141574351665506, -5.166959589539674, 2.5406483216241926, -0.5520516912044007)


def partner(shard, axis, bit):
    return lax.ppermute(shard, axis, [(i, i ^ 1 << bit) for i in range(lax.axis_size(axis))])


def cosine_of_turns(turns, scale):
    rest = turns - jnp.round(turns)
    square = rest * rest
    root = (2.0 * scale) ** 0.5
    half = jnp.float32(SINE[-1] * root)
    for value in SINE[-2::-1]:
        half = half * square + jnp.float32(value * root)
    return jnp.float32(scale) - square * (half * half)


def kernel(
    devices,
    wave_ref,
    taps_ref,
    cell_ref,
    depth_ref,
    slow_ref,
    light_ref,
    aperture_ref,
    out_ref,
    before_ref,
    after_ref,
    mask_ref,
    visiting_ref,
    line_ref,
    filter_ref,
    moved_ref,
    state_ref,
    far_ref,
    table_ref,
    sum_ref,
    arrived_ref,
    send_sem,
    recv_sem,
):
    index = lax.axis_index("space")
    blocks = devices // BOXES
    block_bits = blocks.bit_length() - 1
    box = index // blocks
    block = index % blocks
    count, width = wave_ref.shape
    taps = taps_ref.shape[1]
    reach = (taps - 1) // 2
    halves = count // LANES

    def flipped(value, bit):
        return value + bit - 2 * bit * (value // bit % 2)

    following = (index + blocks) % devices
    previous = (index + devices - blocks) % devices
    mates = [flipped(index, blocks << level) for level in range(LEVELS)]
    paired = [flipped(box, 1 << level) for level in range(LEVELS)]

    def copy(slot, source, target, device):
        return pltpu.make_async_remote_copy(
            src_ref=source,
            dst_ref=target,
            send_sem=send_sem.at[slot],
            recv_sem=recv_sem.at[slot],
            device_id={"space": device},
            device_id_type=pl.DeviceIdType.MESH,
        )

    barrier = pltpu.get_barrier_semaphore()
    for device in [following, previous] + mates:
        pl.semaphore_signal(
            barrier, inc=1, device_id={"space": device}, device_id_type=pl.DeviceIdType.MESH
        )
    pl.semaphore_wait(barrier, LEVELS + 2)

    copies = [
        copy(0, wave_ref.at[:, pl.ds(width - LANES, LANES)], before_ref, following),
        copy(1, wave_ref.at[:, pl.ds(0, LANES)], after_ref, previous),
    ]
    for halo in copies:
        halo.start()

    mask_ref[...] = (aperture_ref[...] > 0).astype(jnp.float32).astype(jnp.bfloat16)
    visit = copy(2, mask_ref, visiting_ref, mates[LEVELS - 1])
    visit.start()
    copies.append(visit)

    for half in range(halves):
        rows = pl.ds(half * LANES, LANES)
        filter_ref[half, :, pl.ds(0, taps)] = taps_ref[
            pl.ds(pl.multiple_of(block * count + half * LANES, LANES), LANES), :
        ]
        filter_ref[half] = filter_ref[half].T
        for part in range(width // LANES):
            piece = wave_ref[rows, pl.ds(part * LANES, LANES)].astype(jnp.float32)
            line_ref[half, pl.ds(reach + part * LANES, LANES), :] = piece.T

    def redatum(half, tile):
        start = pl.multiple_of(tile * TILE, TILE)
        total = jnp.zeros((TILE, LANES), jnp.float32)
        for shift in range(taps):
            total = total + filter_ref[half, pl.ds(shift, 1), :] * line_ref[half, pl.ds(start + shift, TILE), :]
        moved_ref[half, pl.ds(start, TILE), :] = total

    tiles = width // TILE
    edge = (reach + TILE - 1) // TILE

    for half in range(halves):
        pl.loop(edge, tiles - edge)(lambda tile, half=half: redatum(half, tile))
    copies[0].wait_recv()
    copies[1].wait_recv()
    for half in range(halves):
        rows = pl.ds(half * LANES, LANES)
        low = before_ref[rows, :].astype(jnp.float32).T[LANES - reach :, :]
        line_ref[half, pl.ds(0, reach), :] = jnp.where(box > 0, low, jnp.zeros_like(low))
        high = after_ref[rows, :].astype(jnp.float32).T[:reach, :]
        line_ref[half, pl.ds(reach + width, reach), :] = jnp.where(
            box < BOXES - 1, high, jnp.zeros_like(high)
        )
        pl.loop(0, edge)(lambda tile, half=half: redatum(half, tile))
        pl.loop(tiles - edge, tiles)(lambda tile, half=half: redatum(half, tile))
        for part in range(width // LANES):
            columns = pl.ds(part * LANES, LANES)
            state_ref[0, rows, columns] = moved_ref[half, columns, :].T.astype(jnp.bfloat16)

    def fill(slot, level, rows_box, cols_box):
        turn = slow_ref[level] * jnp.float32(0.5 / math.pi)
        across, deep = [], []
        for part in range(width // LANES):
            start = pl.multiple_of(cols_box * width + part * LANES, LANES)
            across.append(cell_ref[pl.ds(level + 1, 1), pl.ds(start, LANES)].astype(jnp.float32) * turn)
            depth = depth_ref[pl.ds(cols_box * (width // LANES) + part, 1), :].astype(jnp.float32) * turn
            deep.append(depth * depth)

        @pl.loop(0, width // LANES)
        def _(group):
            start = pl.multiple_of(rows_box * width + group * LANES, LANES)
            rows = cell_ref[pl.ds(level, 1), pl.ds(start, LANES)].astype(jnp.float32) * turn
            tall = jnp.broadcast_to(rows, (LANES, LANES)).T
            for piece in range(LANES // 16):
                own = tall[piece * 16 : piece * 16 + 16]
                for part in range(width // LANES):
                    apart = own - across[part]
                    sums = apart * apart + deep[part]
                    table = cosine_of_turns(sums * lax.rsqrt(sums), width ** -0.5)
                    table_ref[
                        slot,
                        pl.ds(pl.multiple_of(group * LANES + piece * 16, 16), 16),
                        pl.ds(part * LANES, LANES),
                    ] = table.astype(jnp.bfloat16)

    def term(left, slot, columns):
        return jnp.dot(left, table_ref[slot, :, columns], preferred_element_type=jnp.float32)

    def send(level):
        moving = copy(3 + level, state_ref.at[level], far_ref.at[level], mates[level])
        moving.start()
        copies.append(moving)
        return moving

    last = LEVELS - 1
    plan = [(2 * level + side, level, (box, paired[level])[side], box) for level in range(last) for side in (0, 1)]
    plan += [(2 * last, last, box, paired[last]), (2 * last + 1, last, box, box)]
    ahead = (2, 5, len(plan))
    done = 0
    for level in range(last):
        moving = send(level)
        while done < ahead[level]:
            fill(*plan[done])
            done += 1
        moving.wait_recv()

        @pl.loop(0, width // COLUMNS)
        def _(part):
            columns = pl.ds(pl.multiple_of(part * COLUMNS, COLUMNS), COLUMNS)
            mixed = term(state_ref[level], 2 * level, columns) + term(far_ref[level], 2 * level + 1, columns)
            state_ref[level + 1, :, columns] = mixed.astype(jnp.bfloat16)

    visit.wait_recv()

    @pl.loop(0, width // COLUMNS)
    def _(part):
        columns = pl.ds(pl.multiple_of(part * COLUMNS, COLUMNS), COLUMNS)
        mixed = term(state_ref[last], 2 * last, columns)
        kept = jnp.where(visiting_ref[:, columns].astype(jnp.float32) > 0, mixed, jnp.zeros_like(mixed))
        sum_ref[:, columns] = jnp.sum(kept, 0, keepdims=True)

    final = copy(3 + last, sum_ref, arrived_ref, mates[last])
    final.start()
    copies.append(final)

    @pl.loop(0, width // COLUMNS)
    def _(part):
        columns = pl.ds(pl.multiple_of(part * COLUMNS, COLUMNS), COLUMNS)
        mixed = term(state_ref[last], 2 * last + 1, columns)
        kept = jnp.where(aperture_ref[:, columns] > 0, mixed, jnp.zeros_like(mixed))
        out_ref[:, columns] = jnp.sum(kept, 0, keepdims=True)

    final.wait_recv()
    for part in range(width // LANES):
        columns = pl.ds(part * LANES, LANES)
        weights = light_ref[pl.ds(box * (width // LANES) + part, 1), :]
        both = out_ref[:, columns] + arrived_ref[:, columns]
        out_ref[:, columns] = both * weights * jnp.float32((count * blocks) ** -0.5)
    for moving in copies:
        moving.wait_send()


def on_device(wavefield, redatum_taps, cell_x, cell_depth, slowness, illumination, aperture):
    index = lax.axis_index("space")
    devices = lax.axis_size("space")
    blocks = devices // BOXES
    block_bits = blocks.bit_length() - 1
    count, width = wavefield.shape
    reach = (redatum_taps.shape[1] - 1) // 2
    halves = count // LANES
    vmem = pl.BlockSpec(memory_space=pltpu.VMEM)
    smem = pl.BlockSpec(memory_space=pltpu.SMEM)
    partial_image = pl.pallas_call(
        functools.partial(kernel, devices),
        out_shape=jax.ShapeDtypeStruct((1, width), jnp.float32),
        in_specs=[vmem, vmem, vmem, vmem, smem, vmem, vmem],
        out_specs=vmem,
        scratch_shapes=[
            pltpu.VMEM((count, LANES), jnp.bfloat16),
            pltpu.VMEM((count, LANES), jnp.bfloat16),
            pltpu.VMEM((count, width), jnp.bfloat16),
            pltpu.VMEM((count, width), jnp.bfloat16),
            pltpu.VMEM((halves, width + 2 * reach, LANES), jnp.float32),
            pltpu.VMEM((halves, LANES, LANES), jnp.float32),
            pltpu.VMEM((halves, width, LANES), jnp.float32),
            pltpu.VMEM((LEVELS, count, width), jnp.bfloat16),
            pltpu.VMEM((LEVELS - 1, count, width), jnp.bfloat16),
            pltpu.VMEM((2 * LEVELS, width, width), jnp.bfloat16),
            pltpu.VMEM((1, width), jnp.float32),
            pltpu.VMEM((1, width), jnp.float32),
            pltpu.SemaphoreType.DMA((LEVELS + 3,)),
            pltpu.SemaphoreType.DMA((LEVELS + 3,)),
        ],
        compiler_params=pltpu.CompilerParams(
            collective_id=0, has_side_effects=True, vmem_limit_bytes=60 * 1024 * 1024
        ),
        name="migrate",
    )(
        wavefield,
        redatum_taps,
        cell_x,
        cell_depth.reshape(-1, LANES),
        slowness,
        illumination.reshape(-1, LANES),
        aperture,
    )
    for level in range(block_bits):
        partial_image = partial_image + partner(partial_image, "space", level)
    share = width // blocks
    return lax.dynamic_slice_in_dim(partial_image, index % blocks * share, share, 1)


def solution(mesh):
    placed = (
        P(("groups", "space"), None),
        P("groups", None),
        P(),
        P(),
        P(),
        P("groups"),
        P(("groups", "space"), None),
    )
    return jax.shard_map(
        on_device,
        mesh=mesh,
        in_specs=placed,
        out_specs=P(("groups", "space"), None),
        check_vma=False,
    )
```

profile of v0, /device:TPU:0, one launch (start us, length us, event | category | flops | bytes accessed | tf_op | source)
XLA Modules:
  0.0 59.9 jit_solution(17391265388992198444)
XLA Ops:
  0.0 1.6 %copy.8.taps_ref = f32[256,65]{1,0:T(8,128)} copy(f32[256,65]{0,1:T(8,128)} %param.8) | data formatting | bytes 133120 | tf_op args[1]
  1.6 57.0 %migrate.1 = f32[1,1024]{1,0:T(1,128)} custom-call(bf16[256,1024]{1,0:T(8,128)(2,1)} %wave_ref.1, f32[256,65]{1,0:T(8,128)} %copy.8.taps_ref, s32[5,16384]{1,0:T(8,128)} %cell_ref.1, s32[128,128]{1,0:T(8,128)} %bitcast.2, f32[4]{0:T(128)} %slow_ref.1, f32[128,128]{1,0:T(8,128)} %bitcast.3, s32[256,1024]{1,0:T(8,128)} %aperture_ref.1), custom_call_target="tpu_custom_call" | custom-call | tf_op jit(solution)/shard_map/migrate/pallas_call | solution.py:236
  58.7 1.3 %copy.10 = f32[1,1024]{1,0:T(1,128)} copy(f32[1,1024]{1,0:T(1,128)} %migrate.1) | data formatting | bytes 8192
where the time goes:
time: 60.1 us; the launch traced here: 59.9 us
  Pallas kernels  57 us (95%)
  local copies, waits for them, and re-layouts  2.89 us (5%)
    pallas_call x1, Pallas kernels, on_device(): pl.pallas_call(functools.partial(kernel, devices), out_shape=jax.ShapeDty...  57 us
    unnamed x2, local copies, waits for them, and re-layouts  2.89 us

commit v1 on v0

--- a/solution.py
+++ b/solution.py
@@ -13,7 +13,7 @@
 LANES = 128
 COLUMNS = 256
 TILE = 64
-SINE = (3.141574351665506, -5.166959589539674, 2.5406483216241926, -0.5520516912044007)
+HALF_COSINE = (0.9999982888639185, -4.934458868248177, 4.048770768883701, -1.2477951603331165)
 
 
 def partner(shard, axis, bit):
@@ -24,10 +24,10 @@
     rest = turns - jnp.round(turns)
     square = rest * rest
     root = (2.0 * scale) ** 0.5
-    half = jnp.float32(SINE[-1] * root)
-    for value in SINE[-2::-1]:
+    half = jnp.float32(HALF_COSINE[-1] * root)
+    for value in HALF_COSINE[-2::-1]:
         half = half * square + jnp.float32(value * root)
-    return jnp.float32(scale) - square * (half * half)
+    return half * half - jnp.float32(scale)
 
 
 def kernel(
@@ -45,23 +45,23 @@
     mask_ref,
     visiting_ref,
     line_ref,
-    filter_ref,
-    moved_ref,
-    state_ref,
-    far_ref,
-    table_ref,
+    own_ref,
+    last_ref,
     sum_ref,
     arrived_ref,
     send_sem,
     recv_sem,
+    *large_refs,
 ):
+    tables = large_refs[: 2 * LEVELS]
+    states = large_refs[2 * LEVELS : 3 * LEVELS - 1]
+    fars = large_refs[3 * LEVELS - 1 :]
     index = lax.axis_index("space")
     blocks = devices // BOXES
-    block_bits = blocks.bit_length() - 1
     box = index // blocks
     block = index % blocks
     count, width = wave_ref.shape
-    taps = taps_ref.shape[1]
+    taps = taps_ref.shape[0]
     reach = (taps - 1) // 2
     halves = count // LANES
 
@@ -104,20 +104,17 @@
 
     for half in range(halves):
         rows = pl.ds(half * LANES, LANES)
-        filter_ref[half, :, pl.ds(0, taps)] = taps_ref[
-            pl.ds(pl.multiple_of(block * count + half * LANES, LANES), LANES), :
-        ]
-        filter_ref[half] = filter_ref[half].T
         for part in range(width // LANES):
             piece = wave_ref[rows, pl.ds(part * LANES, LANES)].astype(jnp.float32)
             line_ref[half, pl.ds(reach + part * LANES, LANES), :] = piece.T
 
     def redatum(half, tile):
         start = pl.multiple_of(tile * TILE, TILE)
+        columns = pl.ds(pl.multiple_of(block * count + half * LANES, LANES), LANES)
         total = jnp.zeros((TILE, LANES), jnp.float32)
         for shift in range(taps):
-            total = total + filter_ref[half, pl.ds(shift, 1), :] * line_ref[half, pl.ds(start + shift, TILE), :]
-        moved_ref[half, pl.ds(start, TILE), :] = total
+            total = total + taps_ref[pl.ds(shift, 1), columns] * line_ref[half, pl.ds(start + shift, TILE), :]
+        states[0][pl.ds(start, TILE), pl.ds(half * LANES, LANES)] = total.astype(jnp.bfloat16)
 
     tiles = width // TILE
     edge = (reach + TILE - 1) // TILE
@@ -136,69 +133,81 @@
         )
         pl.loop(0, edge)(lambda tile, half=half: redatum(half, tile))
         pl.loop(tiles - edge, tiles)(lambda tile, half=half: redatum(half, tile))
-        for part in range(width // LANES):
-            columns = pl.ds(part * LANES, LANES)
-            state_ref[0, rows, columns] = moved_ref[half, columns, :].T.astype(jnp.bfloat16)
-
-    def fill(slot, level, rows_box, cols_box):
-        turn = slow_ref[level] * jnp.float32(0.5 / math.pi)
+
+    def fill(table, tall, flat, deep_is_tall, beside=None):
+        turn = slow_ref[min(tall[0], flat[0])] * jnp.float32(0.5 / math.pi)
         across, deep = [], []
         for part in range(width // LANES):
-            start = pl.multiple_of(cols_box * width + part * LANES, LANES)
-            across.append(cell_ref[pl.ds(level + 1, 1), pl.ds(start, LANES)].astype(jnp.float32) * turn)
-            depth = depth_ref[pl.ds(cols_box * (width // LANES) + part, 1), :].astype(jnp.float32) * turn
-            deep.append(depth * depth)
+            start = pl.multiple_of(flat[1] * width + part * LANES, LANES)
+            across.append(cell_ref[pl.ds(flat[0], 1), pl.ds(start, LANES)].astype(jnp.float32) * turn)
+            if not deep_is_tall:
+                depth = depth_ref[pl.ds(flat[1] * (width // LANES) + part, 1), :].astype(jnp.float32) * turn
+                deep.append(depth * depth)
 
         @pl.loop(0, width // LANES)
         def _(group):
-            start = pl.multiple_of(rows_box * width + group * LANES, LANES)
-            rows = cell_ref[pl.ds(level, 1), pl.ds(start, LANES)].astype(jnp.float32) * turn
-            tall = jnp.broadcast_to(rows, (LANES, LANES)).T
+            start = pl.multiple_of(tall[1] * width + group * LANES, LANES)
+            rows = cell_ref[pl.ds(tall[0], 1), pl.ds(start, LANES)].astype(jnp.float32) * turn
+            high = jnp.broadcast_to(rows, (LANES, LANES)).T
+            if deep_is_tall:
+                depth = depth_ref[pl.ds(tall[1] * (width // LANES) + group, 1), :].astype(jnp.float32) * turn
+                sunk = jnp.broadcast_to(depth * depth, (LANES, LANES)).T
             for piece in range(LANES // 16):
-                own = tall[piece * 16 : piece * 16 + 16]
-                for part in range(width // LANES):
-                    apart = own - across[part]
-                    sums = apart * apart + deep[part]
-                    table = cosine_of_turns(sums * lax.rsqrt(sums), width ** -0.5)
-                    table_ref[
-                        slot,
+                own = high[piece * 16 : piece * 16 + 16]
+                for pair in range(width // (2 * LANES)):
+                    both = []
+                    for part in (2 * pair, 2 * pair + 1):
+                        apart = own - across[part]
+                        below = sunk[piece * 16 : piece * 16 + 16] if deep_is_tall else deep[part]
+                        sums = apart * apart + below
+                        both.append(cosine_of_turns(sums * lax.rsqrt(sums), width ** -0.5))
+                    table[
                         pl.ds(pl.multiple_of(group * LANES + piece * 16, 16), 16),
-                        pl.ds(part * LANES, LANES),
-                    ] = table.astype(jnp.bfloat16)
-
-    def term(left, slot, columns):
-        return jnp.dot(left, table_ref[slot, :, columns], preferred_element_type=jnp.float32)
-
-    def send(level):
-        moving = copy(3 + level, state_ref.at[level], far_ref.at[level], mates[level])
+                        pl.ds(pair * 2 * LANES, 2 * LANES),
+                    ] = jnp.concatenate(both, 1).astype(jnp.bfloat16)
+            if beside is not None:
+                beside(pl.ds(pl.multiple_of(group * LANES, LANES), LANES))
+
+    def product(table, rows, right):
+        return jnp.dot(table[rows, :], right[...], preferred_element_type=jnp.float32)
+
+    def own_term(level):
+        def beside(rows):
+            own_ref[rows, :] = product(tables[2 * level], rows, states[level])
+
+        return beside
+
+    last = LEVELS - 1
+    plan = []
+    for level in range(last):
+        for side in (box, paired[level]):
+            plan.append((tables[len(plan)], (level + 1, box), (level, side), True))
+    plan.append((tables[2 * last], (last, box), (last + 1, paired[last]), False))
+    plan.append((tables[2 * last + 1], (last, box), (last + 1, box), False))
+    order = ((0, 1), (2, 3, 4), (5, 6, 7))
+    for level in range(last):
+        moving = copy(3 + level, states[level], fars[level], mates[level])
         moving.start()
         copies.append(moving)
-        return moving
-
-    last = LEVELS - 1
-    plan = [(2 * level + side, level, (box, paired[level])[side], box) for level in range(last) for side in (0, 1)]
-    plan += [(2 * last, last, box, paired[last]), (2 * last + 1, last, box, box)]
-    ahead = (2, 5, len(plan))
-    done = 0
-    for level in range(last):
-        moving = send(level)
-        while done < ahead[level]:
-            fill(*plan[done])
-            done += 1
+        for number in order[level]:
+            fill(*plan[number], own_term(level) if number == 2 * level + (1 if level < last - 1 else 2) else None)
         moving.wait_recv()
 
         @pl.loop(0, width // COLUMNS)
-        def _(part):
-            columns = pl.ds(pl.multiple_of(part * COLUMNS, COLUMNS), COLUMNS)
-            mixed = term(state_ref[level], 2 * level, columns) + term(far_ref[level], 2 * level + 1, columns)
-            state_ref[level + 1, :, columns] = mixed.astype(jnp.bfloat16)
+        def _(part, level=level):
+            rows = pl.ds(pl.multiple_of(part * COLUMNS, COLUMNS), COLUMNS)
+            mixed = own_ref[rows, :] + product(tables[2 * level + 1], rows, fars[level])
+            if level + 1 < last:
+                states[level + 1][rows, :] = mixed.astype(jnp.bfloat16)
+            else:
+                last_ref[:, rows] = mixed.T.astype(jnp.bfloat16)
 
     visit.wait_recv()
 
     @pl.loop(0, width // COLUMNS)
     def _(part):
         columns = pl.ds(pl.multiple_of(part * COLUMNS, COLUMNS), COLUMNS)
-        mixed = term(state_ref[last], 2 * last, columns)
+        mixed = jnp.dot(last_ref[...], tables[2 * last][:, columns], preferred_element_type=jnp.float32)
         kept = jnp.where(visiting_ref[:, columns].astype(jnp.float32) > 0, mixed, jnp.zeros_like(mixed))
         sum_ref[:, columns] = jnp.sum(kept, 0, keepdims=True)
 
@@ -209,7 +218,7 @@
     @pl.loop(0, width // COLUMNS)
     def _(part):
         columns = pl.ds(pl.multiple_of(part * COLUMNS, COLUMNS), COLUMNS)
-        mixed = term(state_ref[last], 2 * last + 1, columns)
+        mixed = jnp.dot(last_ref[...], tables[2 * last + 1][:, columns], preferred_element_type=jnp.float32)
         kept = jnp.where(aperture_ref[:, columns] > 0, mixed, jnp.zeros_like(mixed))
         out_ref[:, columns] = jnp.sum(kept, 0, keepdims=True)
 
@@ -244,23 +253,22 @@
             pltpu.VMEM((count, width), jnp.bfloat16),
             pltpu.VMEM((count, width), jnp.bfloat16),
             pltpu.VMEM((halves, width + 2 * reach, LANES), jnp.float32),
-            pltpu.VMEM((halves, LANES, LANES), jnp.float32),
-            pltpu.VMEM((halves, width, LANES), jnp.float32),
-            pltpu.VMEM((LEVELS, count, width), jnp.bfloat16),
-            pltpu.VMEM((LEVELS - 1, count, width), jnp.bfloat16),
-            pltpu.VMEM((2 * LEVELS, width, width), jnp.bfloat16),
+            pltpu.VMEM((width, count), jnp.float32),
+            pltpu.VMEM((count, width), jnp.bfloat16),
             pltpu.VMEM((1, width), jnp.float32),
             pltpu.VMEM((1, width), jnp.float32),
             pltpu.SemaphoreType.DMA((LEVELS + 3,)),
             pltpu.SemaphoreType.DMA((LEVELS + 3,)),
-        ],
+        ]
+        + [pltpu.VMEM((width, width), jnp.bfloat16)] * (2 * LEVELS)
+        + [pltpu.VMEM((width, count), jnp.bfloat16)] * (2 * LEVELS - 2),
         compiler_params=pltpu.CompilerParams(
             collective_id=0, has_side_effects=True, vmem_limit_bytes=60 * 1024 * 1024
         ),
         name="migrate",
     )(
         wavefield,
-        redatum_taps,
+        redatum_taps.T,
         cell_x,
         cell_depth.reshape(-1, LANES),
         slowness,

time: 60.1 us -> 56.6 us (0.942)
  Pallas kernels: 57 us -> 55.2 us
  local copies, waits for them, and re-layouts: 2.89 us -> 1.28 us
    pallas_call x1, Pallas kernels: 57 us -> 55.2 us  [on_device(): pl.pallas_call(functools.partial(kernel, devices), out_shape=jax.ShapeDty...]
    unnamed x2 -> x1, local copies, waits for them, and re-layouts: 2.89 us -> 1.28 us
where the time goes in v1:
time: 56.6 us; the launch traced here: 56.5 us
  Pallas kernels  55.2 us (98%)
  local copies, waits for them, and re-layouts  1.28 us (2%)
    pallas_call x1, Pallas kernels, on_device(): pl.pallas_call(functools.partial(kernel, devices), out_shape=jax.ShapeDty...  55.2 us
    unnamed x1, local copies, waits for them, and re-layouts  1.28 us

profile of v1, /device:TPU:0, one launch (start us, length us, event | category | flops | bytes accessed | tf_op | source)
XLA Modules:
  0.0 56.5 jit_solution(790718052009341442)
XLA Ops:
  0.0 55.2 %migrate.1 = f32[1,1024]{1,0:T(1,128)} custom-call(bf16[256,1024]{1,0:T(8,128)(2,1)} %wave_ref.1, f32[65,256]{1,0:T(8,128)} %bitcast.3, s32[5,16384]{1,0:T(8,128)} %cell_ref.1, s32[128,128]{1,0:T(8,128)} %bitcast.4, f32[4]{0:T(128)} %slow_ref.1, f32[128,128]{1,0:T(8,128)} %bitcast.5, s32[256,1024]{1,0:T(8,128)} %aperture_ref.1), custom_call_target="tpu_custom_call" | custom-call | tf_op jit(solution)/shard_map/migrate/pallas_call | solution.py:245
  55.2 1.3 %copy.9 = f32[1,1024]{1,0:T(1,128)} copy(f32[1,1024]{1,0:T(1,128)} %migrate.1) | data formatting | bytes 8192
